TPU v7x, 128 devices: a whole 4x4x4 slice. The times are simulated.
128 devices in a mesh: tm: 16 (over z_hi, y, core), space: 8 (over x, z_lo).
Axes of the slice: x: 4, y: 4, z: 4 (z_hi: 2, z_lo: 2; z = z_hi * 2 + z_lo), core: 2. Of those that a mesh axis runs over, the one named last changes fastest.
Arguments:
- tokens: bfloat16 [64, 24, 80, 1024], P('tm', 'space'), may hold values from -6 to 6
- w_in: bfloat16 [1024, 4416], replicated, may hold values from -0.1875 to 0.1875
- w_out: bfloat16 [2048, 1024], replicated, may hold values from -0.125 to 0.125
- a_log_time: float32 [32], replicated, may hold values from -16 to -3
- a_log_space: float32 [32], replicated, may hold values from -14 to -3
- dt_bias_time: float32 [32], replicated, may hold values from -1 to 1
- dt_bias_space: float32 [32], replicated, may hold values from -1 to 1
- skip_time: float32 [32], replicated, may hold values from 0.5 to 1.5
- skip_space: float32 [32], replicated, may hold values from 0.5 to 1.5
- norm_gain: float32 [2048], replicated, may hold values from 0.25 to 1.75
Outputs:
- mixed: bfloat16 [64, 24, 80, 1024], P('tm', 'space')
All inputs are finite; a program needn't handle non-finite values.
Results may differ from a plain program's by a relative error of at most 0.0062.
The roundings to bfloat16 on the way count: a program that leaves them out, or rounds other values in their place, can miss the bound.
Values may be sent and summed in bfloat16 or wider, within the bound.
A program may use at most 192 MiB of HBM per device.

v0:
```python
import jax
import jax.numpy as jnp
from jax import lax
from jax.sharding import PartitionSpec as P

D = 1024
HEADS = 32
HEAD_DIM = 64
STATE = 64
DI = 2048


def from_behind(value, axis, steps):
    count = lax.axis_size(axis)
    leading, last = (max(0, -steps), min(count, count - steps))
    return lax.ppermute(value, axis, [(source, source + steps) for source in range(leading, last)])


def local_scan(inner_seq, inject, readout, log_decay, step_size):
    signal = inner_seq.astype(jnp.float32)
    cum_decay = jnp.cumsum(log_decay, axis=0)
    scores = jnp.dot(readout, inject.T, preferred_element_type=jnp.float32)
    log_span = cum_decay[:, None, :] - cum_decay[None, :, :]
    length = log_decay.shape[0]
    causal = jnp.arange(length)[:, None] >= jnp.arange(length)[None, :]
    decay_mask = jnp.where(causal[:, :, None], jnp.exp(jnp.minimum(log_span, 0.0)), 0.0)
    weights = decay_mask * scores[:, :, None] * step_size[None, :, :]
    local_out = jnp.einsum("srh,rhp->shp", weights, signal, precision=lax.Precision.HIGHEST)
    tail_weight = jnp.exp(cum_decay[-1][None, :] - cum_decay) * step_size
    end_state = jnp.einsum(
        "rhp,rn->hpn",
        tail_weight[:, :, None] * signal,
        inject.astype(jnp.float32),
        precision=lax.Precision.HIGHEST,
    )
    return (local_out, end_state, cum_decay[-1], cum_decay)


def apply_start(local_out, cum_decay, readout, inner_seq, skip_gain, start_state):
    carried = jnp.einsum(
        "sn,hpn->shp", readout.astype(jnp.float32), start_state, precision=lax.Precision.HIGHEST
    )
    return (
        local_out
        + jnp.exp(cum_decay)[:, :, None] * carried
        + skip_gain[None, :, None] * inner_seq.astype(jnp.float32)
    )


def space_carry(end_state, total_decay):
    growth = jnp.exp(total_decay)[..., None, None]

    def relay_step(loop_index, start_state):
        return from_behind(growth * start_state + end_state, "space", 1)

    return lax.fori_loop(0, lax.axis_size("space") - 1, relay_step, jnp.zeros_like(end_state))


def body(
    tokens,
    w_in,
    w_out,
    a_log_time,
    a_log_space,
    dt_bias_time,
    dt_bias_space,
    skip_time,
    skip_space,
    norm_gain,
):
    base = 2 * DI
    w_time = jnp.concatenate(
        [
            w_in[:, DI:base],
            w_in[:, base : base + 2 * STATE],
            w_in[:, base + 4 * STATE : base + 4 * STATE + HEADS],
        ],
        axis=1,
    )
    w_home = jnp.concatenate(
        [
            w_in[:, :DI],
            w_in[:, base + 2 * STATE : base + 4 * STATE],
            w_in[:, base + 4 * STATE + HEADS :],
        ],
        axis=1,
    )
    fr_dev, rows_dev, cols_dev = (tokens.shape[0], tokens.shape[1], tokens.shape[2])
    n_tm = lax.axis_size("tm")
    flat_tokens = tokens.reshape(-1, D)
    home = jnp.dot(flat_tokens, w_home, preferred_element_type=jnp.float32)
    gate_z = home[:, :DI].astype(jnp.bfloat16)
    b_space = home[:, DI : DI + STATE].astype(jnp.bfloat16)
    c_space = home[:, DI + STATE : DI + 2 * STATE].astype(jnp.bfloat16)
    step_space = jax.nn.softplus(home[:, DI + 2 * STATE :] + dt_bias_space)
    decay_space = -jnp.exp(a_log_space) * step_space
    scan_all = jax.vmap(local_scan)
    time_pack = jnp.dot(flat_tokens, w_time, preferred_element_type=jnp.float32).astype(
        jnp.bfloat16
    )
    sending = time_pack.reshape(fr_dev, n_tm, -1, time_pack.shape[-1])
    time_pack = lax.all_to_all(sending, "tm", split_axis=1, concat_axis=0, tiled=True)
    frames = time_pack.shape[0]
    item_count = time_pack.shape[2]
    sequences = jnp.swapaxes(time_pack[:, 0], 0, 1)
    inner_seq = sequences[..., :DI].reshape(item_count, frames, HEADS, HEAD_DIM)
    inject = sequences[..., DI : DI + STATE]
    readout = sequences[..., DI + STATE : DI + 2 * STATE]
    raw_step = sequences[..., DI + 2 * STATE :].astype(jnp.float32)
    step_size = jax.nn.softplus(raw_step + dt_bias_time)
    log_decay = -jnp.exp(a_log_time) * step_size
    time_local_out, unused_end, unused_total, unused_cum = scan_all(
        inner_seq, inject, readout, log_decay, step_size
    )
    result = time_local_out + skip_time[None, None, :, None] * inner_seq.astype(jnp.float32)
    result = result.astype(jnp.bfloat16).reshape(item_count, frames, DI)
    returned = jnp.swapaxes(result, 0, 1)[:, None]
    time_out = lax.all_to_all(returned, "tm", split_axis=0, concat_axis=1, tiled=True)
    space_in = time_out.reshape(fr_dev, rows_dev, cols_dev, HEADS, HEAD_DIM)
    inject_grid = b_space.reshape(fr_dev, rows_dev, cols_dev, STATE)
    readout_grid = c_space.reshape(fr_dev, rows_dev, cols_dev, STATE)
    decay_grid = decay_space.reshape(fr_dev, rows_dev, cols_dev, HEADS)
    step_grid = step_space.reshape(fr_dev, rows_dev, cols_dev, HEADS)
    apply_all = jax.vmap(apply_start, in_axes=(0, 0, 0, 0, None, 0))
    state_now = jnp.zeros((fr_dev, HEADS, HEAD_DIM, STATE), jnp.float32)
    decay_sum = jnp.zeros((fr_dev, HEADS), jnp.float32)
    row_results = []
    row_offsets = []
    for row_index in range(rows_dev):
        inner_row = space_in[:, row_index]
        readout_row = readout_grid[:, row_index]
        local_out, end_state, total_decay, cum_decay = scan_all(
            inner_row,
            inject_grid[:, row_index],
            readout_row,
            decay_grid[:, row_index],
            step_grid[:, row_index],
        )
        row_results.append(
            apply_all(local_out, cum_decay, readout_row, inner_row, skip_space, state_now)
        )
        row_offsets.append(cum_decay + decay_sum[:, None, :])
        state_now = jnp.exp(total_decay)[..., None, None] * state_now + end_state
        decay_sum = decay_sum + total_decay
    space_start = space_carry(state_now, decay_sum)
    finished = []
    for row_index in range(rows_dev):
        carried = jnp.einsum(
            "fsn,fhpn->fshp",
            readout_grid[:, row_index].astype(jnp.float32),
            space_start,
            precision=lax.Precision.HIGHEST,
        )
        finished.append(
            row_results[row_index] + jnp.exp(row_offsets[row_index])[..., None] * carried
        )
    space_out = jnp.stack(finished, axis=1).reshape(-1, DI)
    gated = space_out * jax.nn.silu(gate_z.astype(jnp.float32))
    inv_scale = lax.rsqrt(jnp.mean(gated * gated, axis=-1, keepdims=True) + 1e-05)
    normed = (gated * inv_scale * norm_gain).astype(jnp.bfloat16)
    summed = jnp.dot(normed, w_out, preferred_element_type=jnp.float32) + flat_tokens.astype(
        jnp.float32
    )
    return summed.astype(jnp.bfloat16).reshape(tokens.shape)


def solution(mesh):
    placed = (P("tm", "space", None, None), P(), P(), P(), P(), P(), P(), P(), P(), P())
    return jax.shard_map(
        body, mesh=mesh, in_specs=placed, out_specs=P("tm", "space", None, None), check_vma=False
    )
```

profile of v0, /device:TPU:22, one launch (start us, length us, event | category | flops | bytes accessed | tf_op | source)
XLA Modules:
  0.0 1088.4 jit_solution(10576895644700840184)
XLA Ops:
  3.8 6.4 fusion.41
  10.2 7.3 reshape.156
  17.5 8.0 copy.171
  25.5 8.5 all-to-all-start
  38.7 53.3 %all-to-all-done = bf16[4,16,15,2208]{3,0,2,1:T(4,128)(2,1)} async-done(((bf16[4,16,15,2208]{3,0,2,1:T(4,128)(2,1)}), bf16[4,16,15,2208]{3,0,2,1:T(4,128)(2,1)}, u32[]{:S(2)}, u32[]{:S(2)}) %all-to-all-start) | async-done | bytes 4239392 | tf_op jit(solution)/shard_map/all_to_all | solution.py:102
  92.0 6.4 copy.172
  98.4 7.5 squeeze.58
  105.9 9.3 copy.173
  115.2 7.0 slice.135
  125.0 6.3 fusion.153
  131.6 20.5 %fusion = bf16[15,64,32,64]{1,3,2,0:T(8,128)(2,1)} fusion(bf16[15,64,32,64]{1,3,2,0:T(8,128)(2,1)} %bitcast.194, f32[32]{0:T(128)S(1)} %copy-done.25, f32[15,64,32]{1,2,0:T(8,128)S(1)} %get-tuple-element.43, f32[15,64,64]{2,1,0:T(8,128)S(1)} %fusion.101, f32[15,64,32]{1,2,0:T(8,128)S(1)} %copy.175, pred[64,64]{1,0:T(8,128)(4,1)S(1)} %iota_compare_fusion.1), kind=kOutput, calls=%fused_computation.2 | convolution fusion | flops 1527644160 | bytes 8360064 | tf_op jit(solution)/shard_map/vmap(srh,rhp->shp)/dot_general | solution.py:28
  152.1 10.0 copy.179
  162.1 7.9 all-to-all-start.1
  170.1 9.6 fusion.152
  192.1 32.8 %all-to-all-done.1 = bf16[64,1,15,2048]{3,2,1,0:T(8,128)(2,1)} async-done(((bf16[64,1,15,2048]{3,2,1,0:T(8,128)(2,1)}), bf16[64,1,15,2048]{3,2,1,0:T(8,128)(2,1)}, u32[]{:S(2)}, u32[]{:S(2)}) %all-to-all-start.1) | async-done | bytes 3932192 | tf_op jit(solution)/shard_map/all_to_all | solution.py:118
  234.1 23.2 %reshape.159 = bf16[4,3,80,32,64]{4,3,0,2,1:T(8,128)(2,1)} reshape(bf16[4,16,1,15,2048]{4,0,3,1,2:T(4,128)(2,1)} %copy.181) | data formatting | bytes 7864320 | tf_op jit(solution)/shard_map/reshape | solution.py:119
  257.3 6.1 fusion.149
  297.0 693.8 %while.10 = (s32[]{:T(128)}, f32[4,32,64,64]{3,2,1,0:T(8,128)}, f32[4,32,1,1]{1,0,3,2:T(4,128)S(1)}, f32[4,32,64,64]{3,2,1,0:T(8,128)}, s32[]{:T(128)}) while((s32[]{:T(128)}, f32[4,32,64,64]{3,2,1,0:T(8,128)}, f32[4,32,1,1]{1,0,3,2:T(4,128)S(1)}, f32[4,32,64,64]{3,2,1,0:T(8,128)}, s32[]{:T(128)}) %tuple.48), condition=%wide.region_5.6_spmd, body=%wide.region_4.5_spmd.sunk | while | flops 1048578 | bytes 14680677 | solution.py:56
  305.8 93.0 %collective-permute-done = f32[4,32,64,64]{3,2,1,0:T(8,128)} collective-permute-done((f32[4,32,64,64]{3,2,1,0:T(8,128)}, f32[4,32,64,64]{3,2,1,0:T(8,128)}, u32[]{:S(2)}, u32[]{:S(2)}) %collective-permute-start) | collective-permute-done | bytes 2097184 | tf_op jit(solution)/shard_map/while/body/eval_jaxpr/ppermute | solution.py:16
  406.7 93.0 %collective-permute-done = f32[4,32,64,64]{3,2,1,0:T(8,128)} collective-permute-done((f32[4,32,64,64]{3,2,1,0:T(8,128)}, f32[4,32,64,64]{3,2,1,0:T(8,128)}, u32[]{:S(2)}, u32[]{:S(2)}) %collective-permute-start) | collective-permute-done | bytes 2097184 | tf_op jit(solution)/shard_map/while/body/eval_jaxpr/ppermute | solution.py:16
  507.5 92.2 %collective-permute-done = f32[4,32,64,64]{3,2,1,0:T(8,128)} collective-permute-done((f32[4,32,64,64]{3,2,1,0:T(8,128)}, f32[4,32,64,64]{3,2,1,0:T(8,128)}, u32[]{:S(2)}, u32[]{:S(2)}) %collective-permute-start) | collective-permute-done | bytes 2097184 | tf_op jit(solution)/shard_map/while/body/eval_jaxpr/ppermute | solution.py:16
  607.6 91.3 %collective-permute-done = f32[4,32,64,64]{3,2,1,0:T(8,128)} collective-permute-done((f32[4,32,64,64]{3,2,1,0:T(8,128)}, f32[4,32,64,64]{3,2,1,0:T(8,128)}, u32[]{:S(2)}, u32[]{:S(2)}) %collective-permute-start) | collective-permute-done | bytes 2097184 | tf_op jit(solution)/shard_map/while/body/eval_jaxpr/ppermute | solution.py:16
  706.7 90.4 %collective-permute-done = f32[4,32,64,64]{3,2,1,0:T(8,128)} collective-permute-done((f32[4,32,64,64]{3,2,1,0:T(8,128)}, f32[4,32,64,64]{3,2,1,0:T(8,128)}, u32[]{:S(2)}, u32[]{:S(2)}) %collective-permute-start) | collective-permute-done | bytes 2097184 | tf_op jit(solution)/shard_map/while/body/eval_jaxpr/ppermute | solution.py:16
  804.9 89.5 %collective-permute-done = f32[4,32,64,64]{3,2,1,0:T(8,128)} collective-permute-done((f32[4,32,64,64]{3,2,1,0:T(8,128)}, f32[4,32,64,64]{3,2,1,0:T(8,128)}, u32[]{:S(2)}, u32[]{:S(2)}) %collective-permute-start) | collective-permute-done | bytes 2097184 | tf_op jit(solution)/shard_map/while/body/eval_jaxpr/ppermute | solution.py:16
  902.2 88.5 %collective-permute-done = f32[4,32,64,64]{3,2,1,0:T(8,128)} collective-permute-done((f32[4,32,64,64]{3,2,1,0:T(8,128)}, f32[4,32,64,64]{3,2,1,0:T(8,128)}, u32[]{:S(2)}, u32[]{:S(2)}) %collective-permute-start) | collective-permute-done | bytes 2097184 | tf_op jit(solution)/shard_map/while/body/eval_jaxpr/ppermute | solution.py:16
  1004.6 7.6 fusion.52
  1012.4 7.8 fusion.57
  1020.2 8.1 fusion.61
  1028.4 10.6 pad_maximum_fusion
  1039.0 18.0 %copy.214 = f32[4,3,80,32,64]{4,3,2,1,0:T(8,128)} copy(f32[4,3,80,32,64]{2,4,3,0,1:T(8,128)} %pad_maximum_fusion) | data formatting | bytes 15728640 | tf_op jit(solution)/shard_map/stack | solution.py:157
  1056.9 14.5 %reshape.164 = f32[960,2048]{1,0:T(8,128)} reshape(f32[4,3,80,32,64]{4,3,2,1,0:T(8,128)} %copy.214) | data formatting | bytes 15728640 | tf_op jit(solution)/shard_map/reshape | solution.py:157
  1078.6 9.3 add_convert_fusion
  (126 shorter events, 143.3 us)
Async XLA Ops:
  25.5 66.4 %all-to-all-start = ((bf16[4,16,15,2208]{3,0,2,1:T(4,128)(2,1)}), bf16[4,16,15,2208]{3,0,2,1:T(4,128)(2,1)}, u32[]{:S(2)}, u32[]{:S(2)}) async-start(bf16[4,16,15,2208]{3,0,2,1:T(4,128)(2,1)} %copy.171), calls=%async_computation | async-start | bytes 8847360 | tf_op jit(solution)/shard_map/all_to_all | solution.py:102
  34.0 4.6 copy-start.23
  34.0 4.6 copy-start.24
  115.2 8.4 copy-start.19
  115.2 16.4 %copy-start.25 = (f32[32]{0:T(128)S(1)}, f32[32]{0:T(128)}, u32[]{:S(2)}) copy-start(f32[32]{0:T(128)} %param.19) | copy-start | bytes 388
  162.1 7.9 slice-start.1
  162.1 62.8 %all-to-all-start.1 = ((bf16[64,1,15,2048]{3,2,1,0:T(8,128)(2,1)}), bf16[64,1,15,2048]{3,2,1,0:T(8,128)(2,1)}, u32[]{:S(2)}, u32[]{:S(2)}) async-start(bf16[64,1,15,2048]{3,2,1,0:T(8,128)(2,1)} %bitcast.192), calls=%async_computation.1 | async-start | bytes 8388608 | tf_op jit(solution)/shard_map/all_to_all | solution.py:118
  170.1 9.6 copy-start.18
  302.9 95.9 %collective-permute-start = (f32[4,32,64,64]{3,2,1,0:T(8,128)}, f32[4,32,64,64]{3,2,1,0:T(8,128)}, u32[]{:S(2)}, u32[]{:S(2)}) collective-permute-start(f32[4,32,64,64]{3,2,1,0:T(8,128)} %multiply_add_fusion.4), channel_id=1, source_target_pairs={{0,1},{1,2},{2,3},{3,4},{4,5},{5,6},{6,7},{8,9},{9,10},{10,11},{11... | collective-permute-start | bytes 6291464 | tf_op jit(solution)/shard_map/while/body/eval_jaxpr/ppermute | solution.py:16
  404.6 95.1 %collective-permute-start = (f32[4,32,64,64]{3,2,1,0:T(8,128)}, f32[4,32,64,64]{3,2,1,0:T(8,128)}, u32[]{:S(2)}, u32[]{:S(2)}) collective-permute-start(f32[4,32,64,64]{3,2,1,0:T(8,128)} %multiply_add_fusion.4), channel_id=1, source_target_pairs={{0,1},{1,2},{2,3},{3,4},{4,5},{5,6},{6,7},{8,9},{9,10},{10,11},{11... | collective-permute-start | bytes 6291464 | tf_op jit(solution)/shard_map/while/body/eval_jaxpr/ppermute | solution.py:16
  505.6 94.1 %collective-permute-start = (f32[4,32,64,64]{3,2,1,0:T(8,128)}, f32[4,32,64,64]{3,2,1,0:T(8,128)}, u32[]{:S(2)}, u32[]{:S(2)}) collective-permute-start(f32[4,32,64,64]{3,2,1,0:T(8,128)} %multiply_add_fusion.4), channel_id=1, source_target_pairs={{0,1},{1,2},{2,3},{3,4},{4,5},{5,6},{6,7},{8,9},{9,10},{10,11},{11... | collective-permute-start | bytes 6291464 | tf_op jit(solution)/shard_map/while/body/eval_jaxpr/ppermute | solution.py:16
  605.7 93.2 %collective-permute-start = (f32[4,32,64,64]{3,2,1,0:T(8,128)}, f32[4,32,64,64]{3,2,1,0:T(8,128)}, u32[]{:S(2)}, u32[]{:S(2)}) collective-permute-start(f32[4,32,64,64]{3,2,1,0:T(8,128)} %multiply_add_fusion.4), channel_id=1, source_target_pairs={{0,1},{1,2},{2,3},{3,4},{4,5},{5,6},{6,7},{8,9},{9,10},{10,11},{11... | collective-permute-start | bytes 6291464 | tf_op jit(solution)/shard_map/while/body/eval_jaxpr/ppermute | solution.py:16
  704.8 92.3 %collective-permute-start = (f32[4,32,64,64]{3,2,1,0:T(8,128)}, f32[4,32,64,64]{3,2,1,0:T(8,128)}, u32[]{:S(2)}, u32[]{:S(2)}) collective-permute-start(f32[4,32,64,64]{3,2,1,0:T(8,128)} %multiply_add_fusion.4), channel_id=1, source_target_pairs={{0,1},{1,2},{2,3},{3,4},{4,5},{5,6},{6,7},{8,9},{9,10},{10,11},{11... | collective-permute-start | bytes 6291464 | tf_op jit(solution)/shard_map/while/body/eval_jaxpr/ppermute | solution.py:16
  803.0 91.4 %collective-permute-start = (f32[4,32,64,64]{3,2,1,0:T(8,128)}, f32[4,32,64,64]{3,2,1,0:T(8,128)}, u32[]{:S(2)}, u32[]{:S(2)}) collective-permute-start(f32[4,32,64,64]{3,2,1,0:T(8,128)} %multiply_add_fusion.4), channel_id=1, source_target_pairs={{0,1},{1,2},{2,3},{3,4},{4,5},{5,6},{6,7},{8,9},{9,10},{10,11},{11... | collective-permute-start | bytes 6291464 | tf_op jit(solution)/shard_map/while/body/eval_jaxpr/ppermute | solution.py:16
  900.3 90.5 %collective-permute-start = (f32[4,32,64,64]{3,2,1,0:T(8,128)}, f32[4,32,64,64]{3,2,1,0:T(8,128)}, u32[]{:S(2)}, u32[]{:S(2)}) collective-permute-start(f32[4,32,64,64]{3,2,1,0:T(8,128)} %multiply_add_fusion.4), channel_id=1, source_target_pairs={{0,1},{1,2},{2,3},{3,4},{4,5},{5,6},{6,7},{8,9},{9,10},{10,11},{11... | collective-permute-start | bytes 6291464 | tf_op jit(solution)/shard_map/while/body/eval_jaxpr/ppermute | solution.py:16
  994.7 4.2 copy-start.15
  999.0 5.6 copy-start.1
  999.0 5.6 copy-start.17
  1004.6 7.7 copy-start.4
  1004.6 7.7 copy-start.7
  1004.6 7.7 copy-start.11
  1004.6 7.7 copy-start.12
  1004.6 7.7 copy-start.14
  1012.3 7.9 copy-start.6
  1012.3 7.9 copy-start.8
  1012.3 7.9 copy-start.9
  1012.3 7.9 copy-start.10
  1012.4 7.9 copy-start.13
  1020.2 8.1 copy-start.2
  1071.4 6.7 copy-start
  1071.4 7.2 copy-start.21
  1071.4 7.2 copy-start.22
  (5 other events, 16.8 us)
where the time goes:
time: 1100 us; the launch traced here: 1090 us
  waiting for transfers between devices  724 us (66%)
  local copies, waits for them, and re-layouts  161 us (15%)
  matrix products  105 us (10%)
  other arithmetic  66.9 us (6%)
  starting transfers between devices  30.9 us (3%)
    ppermute x7, waiting for transfers between devices, from_behind(): lax.ppermute(value, axis, [(source, source + steps) for source in range(l...  638 us
    all_to_all x1, waiting for transfers between devices, body(): lax.all_to_all(sending, 'tm', split_axis=1, concat_axis=0, tiled=True)  53.3 us
    dot_general x4, matrix products, local_scan(): jnp.einsum('srh,rhp->shp', weights, signal, precision=lax.Precision.HIGHEST)  42.1 us
    add x7, other arithmetic, relay_step(): return from_behind(growth * start_state + end_state, 'space', 1)  41.3 us
    all_to_all x1, waiting for transfers between devices, body(): lax.all_to_all(returned, 'tm', split_axis=0, concat_axis=1, tiled=True)  32.8 us
    reshape x1, local copies, waits for them, and re-layouts, body(): space_in = time_out.reshape(fr_dev, rows_dev, cols_dev, HEADS, HEAD_DIM)  23.2 us
  transfers between devices with their start and end apart: 9, of which 9 were waited for; matrix products, arithmetic and copies ran while one was open for 2% of the time, Pallas kernels for 0%

commit v1 on v0

--- a/solution.py
+++ b/solution.py
@@ -115,7 +115,10 @@
     result = time_local_out + skip_time[None, None, :, None] * inner_seq.astype(jnp.float32)
     result = result.astype(jnp.bfloat16).reshape(item_count, frames, DI)
     returned = jnp.swapaxes(result, 0, 1)[:, None]
-    time_out = lax.all_to_all(returned, "tm", split_axis=0, concat_axis=1, tiled=True)
+    time_out = jnp.concatenate(
+        lax.all_to_all(jnp.stack(jnp.split(returned, lax.axis_size("tm"), axis=0)), "tm", 0, 0),
+        axis=1,
+    )
     space_in = time_out.reshape(fr_dev, rows_dev, cols_dev, HEADS, HEAD_DIM)
     inject_grid = b_space.reshape(fr_dev, rows_dev, cols_dev, STATE)
     readout_grid = c_space.reshape(fr_dev, rows_dev, cols_dev, STATE)

time: 1100 us -> 1100 us (level)
    unnamed x55 -> x72, local copies, waits for them, and re-layouts: 16.8 us -> 44.6 us
    reshape x1 -> x0, local copies, waits for them, and re-layouts: 23.2 us -> none  [body(): space_in = time_out.reshape(fr_dev, rows_dev, cols_dev, HEADS, HEAD_DIM)]
    another operation x1 -> x3, local copies, waits for them, and re-layouts: 2.55 us -> 16.6 us  [the longest x1 12.2 us: body(): space_in = time_out.reshape(fr_dev, rows_dev, cols_dev, HEADS, HEAD_DIM)]
where the time goes in v1:
time: 1100 us; the launch traced here: 1090 us
  waiting for transfers between devices  720 us (65%)
  local copies, waits for them, and re-layouts  169 us (15%)
  matrix products  104 us (9%)
  other arithmetic  66.9 us (6%)
  starting transfers between devices  30.8 us (3%)
    ppermute x7, waiting for transfers between devices, from_behind(): lax.ppermute(value, axis, [(source, source + steps) for source in range(l...  638 us
    all_to_all x1, waiting for transfers between devices, body(): lax.all_to_all(sending, 'tm', split_axis=1, concat_axis=0, tiled=True)  53.3 us
    unnamed x72, local copies, waits for them, and re-layouts  44.6 us
    dot_general x4, matrix products, local_scan(): jnp.einsum('srh,rhp->shp', weights, signal, precision=lax.Precision.HIGHEST)  42.1 us
    add x7, other arithmetic, relay_step(): return from_behind(growth * start_state + end_state, 'space', 1)  41.3 us
    all_to_all x1, waiting for transfers between devices, body(): lax.all_to_all(jnp.stack(jnp.split(returned, lax.axis_size('tm'), axis=0)...  29.2 us
  transfers between devices with their start and end apart: 9, of which 9 were waited for; matrix products, arithmetic and copies ran while one was open for 2% of the time, Pallas kernels for 0%

profile of v1, /device:TPU:22, one launch (start us, length us, event | category | flops | bytes accessed | tf_op | source)
XLA Modules:
  0.0 1091.7 jit_solution(16451995118966513586)
XLA Ops:
  3.8 6.4 fusion.41
  10.2 7.3 reshape.187
  17.5 8.0 copy.197
  25.5 8.5 all-to-all-start
  38.7 53.3 %all-to-all-done = bf16[4,16,15,2208]{3,0,2,1:T(4,128)(2,1)} async-done(((bf16[4,16,15,2208]{3,0,2,1:T(4,128)(2,1)}), bf16[4,16,15,2208]{3,0,2,1:T(4,128)(2,1)}, u32[]{:S(2)}, u32[]{:S(2)}) %all-to-all-start) | async-done | bytes 4239392 | tf_op jit(solution)/shard_map/all_to_all | solution.py:102
  92.0 6.4 copy.198
  98.3 7.5 squeeze.58
  105.8 9.4 copy.199
  115.2 7.0 slice.151
  125.0 6.3 fusion.169
  131.6 20.5 %fusion = bf16[15,64,32,64]{1,3,2,0:T(8,128)(2,1)} fusion(bf16[15,64,32,64]{1,3,2,0:T(8,128)(2,1)} %bitcast.267, f32[32]{0:T(128)S(1)} %copy-done.26, f32[15,64,32]{1,2,0:T(8,128)S(1)} %get-tuple-element.43, f32[15,64,64]{2,1,0:T(8,128)S(1)} %fusion.117, f32[15,64,32]{1,2,0:T(8,128)S(1)} %copy.201, pred[64,64]{1,0:T(8,128)(4,1)S(1)} %iota_compare_fusion.1), kind=kOutput, calls=%fused_computation.2 | convolution fusion | flops 1527644160 | bytes 8360064 | tf_op jit(solution)/shard_map/vmap(srh,rhp->shp)/dot_general | solution.py:28
  152.1 8.4 copy.205
  190.2 7.9 all-to-all-start.1
  198.1 9.6 fusion.168
  220.2 29.2 %all-to-all-done.1 = bf16[16,4,1,15,2048]{4,1,3,2,0:T(4,128)(2,1)} async-done(((bf16[16,4,1,15,2048]{4,1,3,2,0:T(4,128)(2,1)}), bf16[16,4,1,15,2048]{4,1,3,2,0:T(4,128)(2,1)}, u32[]{:S(2)}, u32[]{:S(2)}) %all-to-all-start.1) | async-done | bytes 3932192 | tf_op jit(solution)/shard_map/all_to_all | solution.py:119
  249.4 12.2 %reshape_reshape.3 = bf16[4,3,80,32,64]{4,3,0,2,1:T(8,128)(2,1)} reshape(bf16[4,16,1,15,2048]{4,0,3,2,1:T(4,128)(2,1)} %bitcast.26) | data formatting | bytes 7864320 | tf_op jit(solution)/shard_map/reshape;reshape | solution.py:122
  261.6 6.1 fusion.165
  297.6 693.8 %while.10 = (s32[]{:T(128)}, f32[4,32,64,64]{3,2,1,0:T(8,128)}, f32[4,32,1,1]{1,0,3,2:T(4,128)S(1)}, f32[4,32,64,64]{3,2,1,0:T(8,128)}, s32[]{:T(128)}) while((s32[]{:T(128)}, f32[4,32,64,64]{3,2,1,0:T(8,128)}, f32[4,32,1,1]{1,0,3,2:T(4,128)S(1)}, f32[4,32,64,64]{3,2,1,0:T(8,128)}, s32[]{:T(128)}) %tuple.48), condition=%wide.region_5.6_spmd, body=%wide.region_4.5_spmd.sunk | while | flops 1048578 | bytes 14680677 | solution.py:56
  306.4 92.9 %collective-permute-done = f32[4,32,64,64]{3,2,1,0:T(8,128)} collective-permute-done((f32[4,32,64,64]{3,2,1,0:T(8,128)}, f32[4,32,64,64]{3,2,1,0:T(8,128)}, u32[]{:S(2)}, u32[]{:S(2)}) %collective-permute-start) | collective-permute-done | bytes 2097184 | tf_op jit(solution)/shard_map/while/body/eval_jaxpr/ppermute | solution.py:16
  407.3 93.0 %collective-permute-done = f32[4,32,64,64]{3,2,1,0:T(8,128)} collective-permute-done((f32[4,32,64,64]{3,2,1,0:T(8,128)}, f32[4,32,64,64]{3,2,1,0:T(8,128)}, u32[]{:S(2)}, u32[]{:S(2)}) %collective-permute-start) | collective-permute-done | bytes 2097184 | tf_op jit(solution)/shard_map/while/body/eval_jaxpr/ppermute | solution.py:16
  508.2 92.2 %collective-permute-done = f32[4,32,64,64]{3,2,1,0:T(8,128)} collective-permute-done((f32[4,32,64,64]{3,2,1,0:T(8,128)}, f32[4,32,64,64]{3,2,1,0:T(8,128)}, u32[]{:S(2)}, u32[]{:S(2)}) %collective-permute-start) | collective-permute-done | bytes 2097184 | tf_op jit(solution)/shard_map/while/body/eval_jaxpr/ppermute | solution.py:16
  608.2 91.3 %collective-permute-done = f32[4,32,64,64]{3,2,1,0:T(8,128)} collective-permute-done((f32[4,32,64,64]{3,2,1,0:T(8,128)}, f32[4,32,64,64]{3,2,1,0:T(8,128)}, u32[]{:S(2)}, u32[]{:S(2)}) %collective-permute-start) | collective-permute-done | bytes 2097184 | tf_op jit(solution)/shard_map/while/body/eval_jaxpr/ppermute | solution.py:16
  707.3 90.4 %collective-permute-done = f32[4,32,64,64]{3,2,1,0:T(8,128)} collective-permute-done((f32[4,32,64,64]{3,2,1,0:T(8,128)}, f32[4,32,64,64]{3,2,1,0:T(8,128)}, u32[]{:S(2)}, u32[]{:S(2)}) %collective-permute-start) | collective-permute-done | bytes 2097184 | tf_op jit(solution)/shard_map/while/body/eval_jaxpr/ppermute | solution.py:16
  805.5 89.5 %collective-permute-done = f32[4,32,64,64]{3,2,1,0:T(8,128)} collective-permute-done((f32[4,32,64,64]{3,2,1,0:T(8,128)}, f32[4,32,64,64]{3,2,1,0:T(8,128)}, u32[]{:S(2)}, u32[]{:S(2)}) %collective-permute-start) | collective-permute-done | bytes 2097184 | tf_op jit(solution)/shard_map/while/body/eval_jaxpr/ppermute | solution.py:16
  902.8 88.5 %collective-permute-done = f32[4,32,64,64]{3,2,1,0:T(8,128)} collective-permute-done((f32[4,32,64,64]{3,2,1,0:T(8,128)}, f32[4,32,64,64]{3,2,1,0:T(8,128)}, u32[]{:S(2)}, u32[]{:S(2)}) %collective-permute-start) | collective-permute-done | bytes 2097184 | tf_op jit(solution)/shard_map/while/body/eval_jaxpr/ppermute | solution.py:16
  1008.0 7.6 fusion.52
  1015.7 8.1 fusion.61
  1023.8 7.9 fusion.57
  1031.7 10.6 pad_maximum_fusion
  1042.3 17.9 %copy.238 = f32[4,3,80,32,64]{4,3,2,1,0:T(8,128)} copy(f32[4,3,80,32,64]{2,4,3,0,1:T(8,128)} %pad_maximum_fusion) | data formatting | bytes 15728640 | tf_op jit(solution)/shard_map/stack | solution.py:160
  1060.2 14.5 %reshape.195 = f32[960,2048]{1,0:T(8,128)} reshape(f32[4,3,80,32,64]{4,3,2,1,0:T(8,128)} %copy.238) | data formatting | bytes 15728640 | tf_op jit(solution)/shard_map/reshape | solution.py:160
  1081.9 9.3 add_convert_fusion
  (142 shorter events, 162.7 us)
Async XLA Ops:
  25.5 66.4 %all-to-all-start = ((bf16[4,16,15,2208]{3,0,2,1:T(4,128)(2,1)}), bf16[4,16,15,2208]{3,0,2,1:T(4,128)(2,1)}, u32[]{:S(2)}, u32[]{:S(2)}) async-start(bf16[4,16,15,2208]{3,0,2,1:T(4,128)(2,1)} %copy.197), calls=%async_computation | async-start | bytes 8847360 | tf_op jit(solution)/shard_map/all_to_all | solution.py:102
  34.0 4.6 copy-start.24
  34.0 4.6 copy-start.25
  115.2 8.4 copy-start.20
  115.2 16.4 %copy-start.26 = (f32[32]{0:T(128)S(1)}, f32[32]{0:T(128)}, u32[]{:S(2)}) copy-start(f32[32]{0:T(128)} %param.19) | copy-start | bytes 388
  188.3 9.8 slice-start.1
  190.2 59.2 %all-to-all-start.1 = ((bf16[16,4,1,15,2048]{4,1,3,2,0:T(4,128)(2,1)}), bf16[16,4,1,15,2048]{4,1,3,2,0:T(4,128)(2,1)}, u32[]{:S(2)}, u32[]{:S(2)}) async-start(bf16[16,4,1,15,2048]{4,1,3,2,0:T(4,128)(2,1)} %fusion.101), calls=%async_computation.1 | async-start | bytes 7864320 | tf_op jit(solution)/shard_map/all_to_all | solution.py:119
  198.1 9.6 copy-start.19
  287.6 3.6 copy-start.7
  303.5 95.9 %collective-permute-start = (f32[4,32,64,64]{3,2,1,0:T(8,128)}, f32[4,32,64,64]{3,2,1,0:T(8,128)}, u32[]{:S(2)}, u32[]{:S(2)}) collective-permute-start(f32[4,32,64,64]{3,2,1,0:T(8,128)} %multiply_add_fusion.4), channel_id=1, source_target_pairs={{0,1},{1,2},{2,3},{3,4},{4,5},{5,6},{6,7},{8,9},{9,10},{10,11},{11... | collective-permute-start | bytes 6291464 | tf_op jit(solution)/shard_map/while/body/eval_jaxpr/ppermute | solution.py:16
  405.3 95.1 %collective-permute-start = (f32[4,32,64,64]{3,2,1,0:T(8,128)}, f32[4,32,64,64]{3,2,1,0:T(8,128)}, u32[]{:S(2)}, u32[]{:S(2)}) collective-permute-start(f32[4,32,64,64]{3,2,1,0:T(8,128)} %multiply_add_fusion.4), channel_id=1, source_target_pairs={{0,1},{1,2},{2,3},{3,4},{4,5},{5,6},{6,7},{8,9},{9,10},{10,11},{11... | collective-permute-start | bytes 6291464 | tf_op jit(solution)/shard_map/while/body/eval_jaxpr/ppermute | solution.py:16
  506.2 94.1 %collective-permute-start = (f32[4,32,64,64]{3,2,1,0:T(8,128)}, f32[4,32,64,64]{3,2,1,0:T(8,128)}, u32[]{:S(2)}, u32[]{:S(2)}) collective-permute-start(f32[4,32,64,64]{3,2,1,0:T(8,128)} %multiply_add_fusion.4), channel_id=1, source_target_pairs={{0,1},{1,2},{2,3},{3,4},{4,5},{5,6},{6,7},{8,9},{9,10},{10,11},{11... | collective-permute-start | bytes 6291464 | tf_op jit(solution)/shard_map/while/body/eval_jaxpr/ppermute | solution.py:16
  606.3 93.2 %collective-permute-start = (f32[4,32,64,64]{3,2,1,0:T(8,128)}, f32[4,32,64,64]{3,2,1,0:T(8,128)}, u32[]{:S(2)}, u32[]{:S(2)}) collective-permute-start(f32[4,32,64,64]{3,2,1,0:T(8,128)} %multiply_add_fusion.4), channel_id=1, source_target_pairs={{0,1},{1,2},{2,3},{3,4},{4,5},{5,6},{6,7},{8,9},{9,10},{10,11},{11... | collective-permute-start | bytes 6291464 | tf_op jit(solution)/shard_map/while/body/eval_jaxpr/ppermute | solution.py:16
  705.4 92.3 %collective-permute-start = (f32[4,32,64,64]{3,2,1,0:T(8,128)}, f32[4,32,64,64]{3,2,1,0:T(8,128)}, u32[]{:S(2)}, u32[]{:S(2)}) collective-permute-start(f32[4,32,64,64]{3,2,1,0:T(8,128)} %multiply_add_fusion.4), channel_id=1, source_target_pairs={{0,1},{1,2},{2,3},{3,4},{4,5},{5,6},{6,7},{8,9},{9,10},{10,11},{11... | collective-permute-start | bytes 6291464 | tf_op jit(solution)/shard_map/while/body/eval_jaxpr/ppermute | solution.py:16
  803.6 91.4 %collective-permute-start = (f32[4,32,64,64]{3,2,1,0:T(8,128)}, f32[4,32,64,64]{3,2,1,0:T(8,128)}, u32[]{:S(2)}, u32[]{:S(2)}) collective-permute-start(f32[4,32,64,64]{3,2,1,0:T(8,128)} %multiply_add_fusion.4), channel_id=1, source_target_pairs={{0,1},{1,2},{2,3},{3,4},{4,5},{5,6},{6,7},{8,9},{9,10},{10,11},{11... | collective-permute-start | bytes 6291464 | tf_op jit(solution)/shard_map/while/body/eval_jaxpr/ppermute | solution.py:16
  900.9 90.5 %collective-permute-start = (f32[4,32,64,64]{3,2,1,0:T(8,128)}, f32[4,32,64,64]{3,2,1,0:T(8,128)}, u32[]{:S(2)}, u32[]{:S(2)}) collective-permute-start(f32[4,32,64,64]{3,2,1,0:T(8,128)} %multiply_add_fusion.4), channel_id=1, source_target_pairs={{0,1},{1,2},{2,3},{3,4},{4,5},{5,6},{6,7},{8,9},{9,10},{10,11},{11... | collective-permute-start | bytes 6291464 | tf_op jit(solution)/shard_map/while/body/eval_jaxpr/ppermute | solution.py:16
  995.3 4.4 copy-start.1
  1002.3 5.6 copy-start.3
  1002.3 5.6 copy-start.18
  1007.9 7.7 copy-start.8
  1007.9 7.7 copy-start.9
  1007.9 7.7 copy-start.13
  1008.0 7.7 copy-start.14
  1008.0 7.7 copy-start.15
  1015.6 8.2 copy-start.6
  1015.6 8.2 copy-start.10
  1015.7 8.1 copy-start.11
  1015.7 8.1 copy-start.12
  1023.8 7.9 copy-start.4
  1074.7 6.7 copy-start.2
  1074.7 7.2 copy-start.22
  1074.7 7.2 copy-start.23
  (6 other events, 15.4 us)
